TPU v7x, 32 devices: a whole 2x2x4 slice. The times are simulated.
32 devices in a mesh: row: 2 (over core), col: 4 (over z), ind: 4 (over y, x).
Axes of the slice: x: 2, y: 2, z: 4, core: 2. Of those that a mesh axis runs over, the one named last changes fastest.
Arguments:
- dosages: bfloat16 [4096, 1024], P('ind', ('row', 'col'))
- annotations: bfloat16 [1024, 1024], P('ind', ('row', 'col')), may hold values from -6 to 6
- window_end: int32 [1024], P(('row', 'col')), may hold values from 512 to 1024, as said below
Outputs:
- ld_scores: float32 [1024, 1024], P('ind', ('row', 'col'))
Inputs may be any that keep to these rules, and one draw needn't show every extreme that they name: window_end is nondecreasing, window_end[j] > j, and window_end[j] <= min(1024, (j // 128 + 4) * 128), the last bound reached in every draw.
All inputs are finite; a program needn't handle non-finite values.
Results may differ from a plain program's by a relative error of at most 0.0029.
Values may be sent and summed in bfloat16 or wider, within the bound.
A program may use at most 64 MiB of HBM per device.

v0:
```python
import jax
import jax.numpy as jnp
from jax import lax
from jax.sharding import PartitionSpec as P


def from_behind(array, axis, by):
    count = lax.axis_size(axis)
    pairs = [(i, i + by) for i in range(count) if 0 <= i + by < count]
    return lax.ppermute(array, axis, pairs)


def per_device(dosages, annotations, window_end):
    band_count = lax.axis_size("col")
    column_index = lax.axis_index("col")
    tile_size = dosages.shape[1]
    ind_rows = dosages.shape[0]
    ann_rows = annotations.shape[0]
    group_width = band_count * tile_size
    sample_count = ind_rows * lax.axis_size("ind")
    window_ends = lax.all_gather(window_end, "col", axis=0, tiled=True)
    group_x, group_a = (
        lax.all_gather(dosages, "col", axis=1, tiled=True),
        lax.all_gather(annotations, "col", axis=1, tiled=True),
    )
    next_x, next_a = from_behind((group_x, group_a), "row", -1)
    wide_x = jnp.concatenate([group_x, next_x], axis=1)
    wide_a = jnp.concatenate([group_a, next_a], axis=1)
    band_x = lax.dynamic_slice_in_dim(wide_x, column_index * tile_size, group_width, 1)
    band_a = lax.dynamic_slice_in_dim(wide_a, column_index * tile_size, group_width, 1)
    rows_x = group_x.reshape(ind_rows, band_count, tile_size)
    cols_x = band_x.reshape(ind_rows, band_count, tile_size)
    partial_gram = jnp.einsum("inb,ine->nbe", rows_x, cols_x, preferred_element_type=jnp.float32)
    gram = lax.psum(partial_gram, "ind")
    correlation_matrix = gram / sample_count
    raw_rsquared = correlation_matrix * correlation_matrix
    unbiased_rsquared = raw_rsquared - (1.0 - raw_rsquared) / (sample_count - 2)
    group_start = lax.axis_index("row") * group_width
    block_ids = jnp.arange(band_count, dtype=jnp.int32)[:, None, None]
    within_window = jnp.arange(tile_size, dtype=jnp.int32)
    row_pos = group_start + block_ids * tile_size + within_window[None, :, None]
    col_pos = group_start + (block_ids + column_index) * tile_size + within_window[None, None, :]
    limit = window_ends.reshape(band_count, tile_size)[:, :, None]
    inside = col_pos < limit
    upper = jnp.where((col_pos >= row_pos) & inside, unbiased_rsquared, 0.0).astype(jnp.bfloat16)
    strict = jnp.where((col_pos > row_pos) & inside, unbiased_rsquared, 0.0).astype(jnp.bfloat16)
    annotation_rows = group_a.reshape(ann_rows, band_count, tile_size)
    cols_a = band_a.reshape(ann_rows, band_count, tile_size)
    direct = jnp.einsum("cne,nae->cna", cols_a, upper, preferred_element_type=jnp.float32)
    mirror = jnp.einsum("cna,nae->cne", annotation_rows, strict, preferred_element_type=jnp.float32)
    direct = direct.reshape(ann_rows, group_width)
    mirror = mirror.reshape(ann_rows, group_width)
    window_acc = jnp.zeros((ann_rows, 2 * group_width), jnp.float32)
    window_acc = lax.dynamic_update_slice_in_dim(window_acc, mirror, column_index * tile_size, 1)
    window_acc = window_acc.at[:, :group_width].add(direct)
    incoming = from_behind(window_acc[:, group_width:], "row", 1)
    combined = window_acc[:, :group_width] + incoming
    ld_scores = lax.psum_scatter(combined, "col", scatter_dimension=1, tiled=True)
    return ld_scores


def solution(mesh):
    in_specs = (P("ind", ("row", "col")), P("ind", ("row", "col")), P(("row", "col")))
    out_specs = P("ind", ("row", "col"))
    return jax.shard_map(
        per_device, mesh=mesh, in_specs=in_specs, out_specs=out_specs, check_vma=False
    )
```

profile of v0, /device:TPU:0, one launch (start us, length us, event | category | flops | bytes accessed | tf_op | source)
XLA Modules:
  0.0 139.3 jit_solution(7500563988074717324)
XLA Ops:
  6.5 0.0 all-gather.3.cloned.1.call-start
  6.5 1.8 %copy.16 = bf16[1024,128]{0,1:T(8,128)(2,1)} copy(bf16[1024,128]{1,0:T(8,128)(2,1)} %param.5) | data formatting | bytes 524288 | tf_op args[0]
  8.3 0.0 all-gather.3.cloned.1.call-update
  8.4 0.0 all-reduce.2.cloned.1.call-start
  8.4 31.2 %all-gather.3.cloned.1.call-done = bf16[1024,512]{0,1:T(8,128)(2,1)} async-done(((bf16[1024,128]{0,1:T(8,128)(2,1)}), bf16[1024,512]{0,1:T(8,128)(2,1)}) %all-gather.3.cloned.1.call-update) | async-done | bytes 1048592 | tf_op jit(solution)/shard_map/all_gather | solution.py:23
  39.6 1.3 collective-permute-start
  40.9 0.9 copy.18
  41.9 14.4 %all_gather.11 = bf16[256,512]{0,1:T(8,128)(2,1)S(1)} all-gather(bf16[256,128]{0,1:T(8,128)(2,1)S(1)} %copy.18), channel_id=1, replica_groups=mesh['row'=2,'col'=4,'ind'=4] {'col'}, dimensions={1}, use_global_device_ids=true | all-gather | bytes 327680 | tf_op jit(solution)/shard_map/all_gather | solution.py:24
  56.2 1.3 collective-permute-start.1
  57.6 0.0 copy-start
  57.6 0.0 collective-permute-done
  57.6 2.3 %fusion = bf16[1024,512]{0,1:T(8,128)(2,1)S(1)} fusion(s32[]{:T(128)S(6)} %select_n.12, bf16[1024,512]{0,1:T(8,128)(2,1)} %all-gather.3.cloned.1.call-done, bf16[1024,512]{0,1:T(8,128)(2,1)S(1)} %collective-permute-done), kind=kLoop, calls=%fused_computation.3 | loop fusion | flops 2097152 | bytes 3145732 | tf_op jit(solution)/shard_map/concatenate | solution.py:27
  59.9 0.0 copy-done
  59.9 0.0 copy-start.2
  59.9 1.1 convolution_bitcast_fusion
  61.0 0.0 all-reduce.2.cloned.1.call-update
  61.1 0.0 reduce-scatter.2.cloned.1.call-start
  61.1 0.1 iota_add_fusion
  61.2 0.0 copy-done.2
  61.2 9.1 %all-gather = s32[4,1,128]{2,1,0:T(1,128)S(1)} all-gather(s32[1,1,128]{2,1,0:T(1,128)S(1)} %bitcast.26), channel_id=1, replica_groups=mesh['row'=2,'col'=4,'ind'=4] {'col'}, dimensions={0}, use_global_device_ids=true | all-gather | bytes 2560 | tf_op jit(solution)/shard_map/all_gather | solution.py:21
  70.3 0.1 iota_add_fusion.1
  70.3 33.8 %all-reduce.2.cloned.1.call-done = f32[4,128,128]{1,2,0:T(8,128)} async-done(((f32[4,128,128]{1,2,0:T(8,128)}), f32[4,128,128]{1,2,0:T(8,128)}) %all-reduce.2.cloned.1.call-update) | async-done | bytes 262160 | tf_op jit(solution)/shard_map/psum | solution.py:34
  104.2 1.2 fusion.3
  105.4 0.2 copy.20
  105.6 0.1 broadcast_in_dim.11
  105.7 0.1 constant_dynamic-update-slice_fusion
  105.8 0.0 copy-start.1
  105.8 1.5 %collective-permute-start.2 = (f32[256,512]{1,0:T(8,128)S(1)}, f32[256,512]{1,0:T(8,128)S(1)}, u32[]{:S(2)}, u32[]{:S(2)}) collective-permute-start(f32[256,512]{1,0:T(8,128)S(1)} %slice.29), channel_id=1, source_target_pairs={{0,16},{1,17},{2,18},{3,19},{4,20},{5,21},{6,22},{7,23},{8,24},{9,... | collective-permute-start | bytes 1572872 | tf_op jit(solution)/shard_map/ppermute | solution.py:10
  107.3 0.6 compare_reduce_fusion
  107.9 0.0 collective-permute-done.1
  107.9 0.6 fusion.2
  108.6 0.0 copy-done.1
  108.6 0.4 fusion.4
  108.9 0.2 copy.23
  109.1 0.0 collective-permute-done.2
  109.1 1.6 %fusion.1 = f32[256,512]{1,0:T(8,128)} fusion(f32[256,512]{1,0:T(8,128)S(1)} %collective-permute-done.2, f32[256,512]{1,0:T(8,128)S(1)} %copy.23, f32[256,1024]{1,0:T(8,128)S(1)} %constant_dynamic-update-slice_fusion, pred[]{:T(512)} %compare_reduce_fusion), kind=kLoop, calls=%fused_computation.5 | loop fusion | flops 393216 | bytes 2097153 | tf_op jit(solution)/shard_map/add | solution.py:57
  110.7 0.0 reduce-scatter.2.cloned.1.call-update
  110.8 22.0 %reduce-scatter.2.cloned.1.call-done = f32[256,128]{1,0:T(8,128)} async-done(((f32[256,512]{1,0:T(8,128)}), f32[256,128]{1,0:T(8,128)}) %reduce-scatter.2.cloned.1.call-update) | async-done | bytes 131088 | tf_op jit(solution)/shard_map/reduce_scatter | solution.py:58
  (2 shorter events, 0.0 us)
Async XLA Ops:
  6.5 33.1 %all-gather.3.cloned.1.call-start = ((), (), s32[]{:S(2)}) async-start(), calls=%async_computation.1 | async-start | bytes 1310720 | tf_op jit(solution)/shard_map/all_gather | solution.py:23
  8.4 95.8 %all-reduce.2.cloned.1.call-start = ((), (), s32[]{:S(2)}) async-start(), calls=%async_computation.2 | async-start | bytes 524288 | tf_op jit(solution)/shard_map/psum | solution.py:34
  39.6 17.9 %collective-permute-start = (bf16[1024,512]{0,1:T(8,128)(2,1)}, bf16[1024,512]{0,1:T(8,128)(2,1)S(1)}, u32[]{:S(2)}, u32[]{:S(2)}) collective-permute-start(bf16[1024,512]{0,1:T(8,128)(2,1)} %all-gather.3.cloned.1.call-done), channel_id=1, source_target_pairs={{16,0},{17,1},{18,2},{19,3},{20,4},{21,5},{22,6},{23,7},{24,8},{25... | collective-permute-start | bytes 3145736 | tf_op jit(solution)/shard_map/ppermute | solution.py:10
  56.2 51.7 %collective-permute-start.1 = (bf16[256,512]{0,1:T(8,128)(2,1)S(1)}, bf16[256,512]{0,1:T(8,128)(2,1)S(1)}, u32[]{:S(2)}, u32[]{:S(2)}) collective-permute-start(bf16[256,512]{0,1:T(8,128)(2,1)S(1)} %all_gather.11), channel_id=1, source_target_pairs={{16,0},{17,1},{18,2},{19,3},{20,4},{21,5},{22,6},{23,7},{24,8},{25... | collective-permute-start | bytes 786440 | tf_op jit(solution)/shard_map/ppermute | solution.py:10
  57.6 2.3 %copy-start = (bf16[1024,512]{0,1:T(8,128)(2,1)S(1)}, bf16[1024,512]{0,1:T(8,128)(2,1)}, u32[]{:S(2)}) copy-start(bf16[1024,512]{0,1:T(8,128)(2,1)} %all-gather.3.cloned.1.call-done) | copy-start | bytes 3145732
  59.9 1.3 copy-start.2
  61.1 71.7 %reduce-scatter.2.cloned.1.call-start = ((), (), s32[]{:S(2)}) async-start(), calls=%async_computation.3 | async-start | bytes 655360 | tf_op jit(solution)/shard_map/reduce_scatter | solution.py:58
  105.8 2.8 %copy-start.1 = (f32[4,128,128]{1,2,0:T(8,128)S(1)}, f32[4,128,128]{1,2,0:T(8,128)}, u32[]{:S(2)}) copy-start(f32[4,128,128]{1,2,0:T(8,128)} %all-reduce.2.cloned.1.call-done) | copy-start | bytes 786436
  105.8 3.3 %collective-permute-start.2 = (f32[256,512]{1,0:T(8,128)S(1)}, f32[256,512]{1,0:T(8,128)S(1)}, u32[]{:S(2)}, u32[]{:S(2)}) collective-permute-start(f32[256,512]{1,0:T(8,128)S(1)} %slice.29), channel_id=1, source_target_pairs={{0,16},{1,17},{2,18},{3,19},{4,20},{5,21},{6,22},{7,23},{8,24},{9,... | collective-permute-start | bytes 1572872 | tf_op jit(solution)/shard_map/ppermute | solution.py:10
Sparse Core Ops, SparseCore 0:
  8.9 30.6 all-gather.2
  61.2 42.9 all-reduce.1
  110.9 21.8 reduce-scatter.1
where the time goes:
time: 140 us; the launch traced here: 139 us
  waiting for transfers between devices  87.1 us (62%)
  blocking collectives  23.5 us (17%)
  between operations  13.3 us (10%)
  other arithmetic  5.3 us (4%)
  starting transfers between devices  4.1 us (3%)
  local copies, waits for them, and re-layouts  3.35 us (2%)
  matrix products  2.71 us (2%)
    psum x1, waiting for transfers between devices, per_device(): gram = lax.psum(partial_gram, 'ind')  33.8 us
    all_gather x1, waiting for transfers between devices, per_device(): lax.all_gather(dosages, 'col', axis=1, tiled=True)  31.2 us
    reduce_scatter x1, waiting for transfers between devices, per_device(): lax.psum_scatter(combined, 'col', scatter_dimension=1, tiled=True)  22 us
    all_gather x1, blocking collectives, per_device(): lax.all_gather(annotations, 'col', axis=1, tiled=True)  14.4 us
    all_gather x1, blocking collectives, per_device(): window_ends = lax.all_gather(window_end, 'col', axis=0, tiled=True)  9.09 us
    ppermute x3, starting transfers between devices, from_behind(): return lax.ppermute(array, axis, pairs)  4.02 us
  transfers between devices with their start and end apart: 6, of which 3 were waited for; matrix products, arithmetic and copies ran while one was open for 6% of the time, Pallas kernels for 0%

commit v1 on v0

--- a/solution.py
+++ b/solution.py
@@ -18,7 +18,12 @@
     ann_rows = annotations.shape[0]
     group_width = band_count * tile_size
     sample_count = ind_rows * lax.axis_size("ind")
-    window_ends = lax.all_gather(window_end, "col", axis=0, tiled=True)
+    ring = [window_end]
+    for hop in range(3):
+        ring.append(lax.ppermute(ring[-1], "col", [(dev, (dev + 1) % 4) for dev in range(4)]))
+    window_ends = jnp.roll(
+        jnp.concatenate(ring[::-1], axis=0), (lax.axis_index("col") + 1) * ring[0].shape[0], axis=0
+    )
     group_x, group_a = (
         lax.all_gather(dosages, "col", axis=1, tiled=True),
         lax.all_gather(annotations, "col", axis=1, tiled=True),

time: 140 us -> 134 us (0.957)
  blocking collectives: 23.5 us -> 16.2 us
  starting transfers between devices: 4.1 us -> 8 us
  waiting for transfers between devices: 87.1 us -> 84.5 us
    all_gather x1, waiting for transfers between devices: 31.2 us -> 11 us  [per_device(): lax.all_gather(dosages, 'col', axis=1, tiled=True)]
    ppermute x0 -> x3, waiting for transfers between devices: none -> 9.94 us  [per_device(): lax.ppermute(ring[-1], 'col', [(dev, (dev + 1) % 4) for dev in range(4)])]
    all_gather x1 -> x0, blocking collectives: 9.09 us -> none  [per_device(): window_ends = lax.all_gather(window_end, 'col', axis=0, tiled=True)]
    psum x1, waiting for transfers between devices: 33.8 us -> 41.4 us  [per_device(): gram = lax.psum(partial_gram, 'ind')]
    ppermute x0 -> x3, starting transfers between devices: none -> 3.9 us  [per_device(): lax.ppermute(ring[-1], 'col', [(dev, (dev + 1) % 4) for dev in range(4)])]
    all_gather x1, blocking collectives: 14.4 us -> 16.2 us  [per_device(): lax.all_gather(annotations, 'col', axis=1, tiled=True)]
    unnamed x8 -> x15, local copies, waits for them, and re-layouts: 2.74 us -> 2.81 us
  transfers between devices with their start and end apart: 6 -> 9, of which waited for: 3 -> 5; matrix products, arithmetic and copies ran while one was open for 6% -> 6% of each run, Pallas kernels for 0% -> 0%
where the time goes in v1:
time: 134 us; the launch traced here: 133 us
  waiting for transfers between devices  84.5 us (63%)
  blocking collectives  16.2 us (12%)
  between operations  13.3 us (10%)
  starting transfers between devices  8 us (6%)
  other arithmetic  5.3 us (4%)
  local copies, waits for them, and re-layouts  3.49 us (3%)
  matrix products  2.71 us (2%)
    psum x1, waiting for transfers between devices, per_device(): gram = lax.psum(partial_gram, 'ind')  41.4 us
    reduce_scatter x1, waiting for transfers between devices, per_device(): lax.psum_scatter(combined, 'col', scatter_dimension=1, tiled=True)  22 us
    all_gather x1, blocking collectives, per_device(): lax.all_gather(annotations, 'col', axis=1, tiled=True)  16.2 us
    all_gather x1, waiting for transfers between devices, per_device(): lax.all_gather(dosages, 'col', axis=1, tiled=True)  11 us
    ppermute x3, waiting for transfers between devices, per_device(): lax.ppermute(ring[-1], 'col', [(dev, (dev + 1) % 4) for dev in range(4)])  9.94 us
    ppermute x3, starting transfers between devices, from_behind(): return lax.ppermute(array, axis, pairs)  4.02 us
    ppermute x3, starting transfers between devices, per_device(): lax.ppermute(ring[-1], 'col', [(dev, (dev + 1) % 4) for dev in range(4)])  3.9 us
    unnamed x15, local copies, waits for them, and re-layouts  2.81 us
  transfers between devices with their start and end apart: 9, of which 5 were waited for; matrix products, arithmetic and copies ran while one was open for 6% of the time, Pallas kernels for 0%

profile of v1, /device:TPU:0, one launch (start us, length us, event | category | flops | bytes accessed | tf_op | source)
XLA Modules:
  0.0 133.5 jit_solution(1246180010778010427)
XLA Ops:
  6.5 0.0 copy-start.2
  6.5 0.0 all-gather.2.cloned.1.call-start
  6.5 1.8 %copy.8 = bf16[1024,128]{0,1:T(8,128)(2,1)} copy(bf16[1024,128]{1,0:T(8,128)(2,1)} %param.5) | data formatting | bytes 524288 | tf_op args[0]
  8.3 0.0 all-gather.2.cloned.1.call-update
  8.4 0.0 all-reduce.2.cloned.1.call-start
  8.4 3.1 %collective-permute-start = (s32[128]{0:T(128)}, s32[128]{0:T(128)S(1)}, u32[]{:S(2)}, u32[]{:S(2)}) collective-permute-start(s32[128]{0:T(128)} %param.7), channel_id=1, source_target_pairs={{0,4},{4,8},{8,12},{12,0},{1,5},{5,9},{9,13},{13,1},{2,6},{6,10},{... | collective-permute-start | bytes 1544 | tf_op jit(solution)/shard_map/ppermute | solution.py:23
  11.5 0.9 copy.10
  12.5 16.2 %all_gather.7 = bf16[256,512]{0,1:T(8,128)(2,1)S(1)} all-gather(bf16[256,128]{0,1:T(8,128)(2,1)S(1)} %copy.10), channel_id=1, replica_groups=mesh['row'=2,'col'=4,'ind'=4] {'col'}, dimensions={1}, use_global_device_ids=true | all-gather | bytes 327680 | tf_op jit(solution)/shard_map/all_gather | solution.py:29
  28.7 1.3 collective-permute-start.4
  30.0 11.0 %all-gather.2.cloned.1.call-done = bf16[1024,512]{0,1:T(8,128)(2,1)} async-done(((bf16[1024,128]{0,1:T(8,128)(2,1)}), bf16[1024,512]{0,1:T(8,128)(2,1)}) %all-gather.2.cloned.1.call-update) | async-done | bytes 1048592 | tf_op jit(solution)/shard_map/all_gather | solution.py:28
  41.0 1.3 collective-permute-start.3
  42.3 0.1 iota_add_fusion
  42.4 0.1 iota_add_fusion.1
  42.4 0.0 collective-permute-done
  42.4 0.8 collective-permute-start.1
  43.2 4.6 %collective-permute-done.1 = s32[128]{0:T(128)S(1)} collective-permute-done((s32[128]{0:T(128)S(1)}, s32[128]{0:T(128)S(1)}, u32[]{:S(2)}, u32[]{:S(2)}) %collective-permute-start.1) | collective-permute-done | bytes 544 | tf_op jit(solution)/shard_map/ppermute | solution.py:23
  47.8 0.0 collective-permute-start.2
  47.8 5.4 %collective-permute-done.2 = s32[128]{0:T(128)S(1)} collective-permute-done((s32[128]{0:T(128)S(1)}, s32[128]{0:T(128)S(1)}, u32[]{:S(2)}, u32[]{:S(2)}) %collective-permute-start.2) | collective-permute-done | bytes 544 | tf_op jit(solution)/shard_map/ppermute | solution.py:23
  53.2 0.0 copy-done.2
  53.2 0.0 copy-start
  53.3 0.0 collective-permute-done.3
  53.3 2.3 %fusion = bf16[1024,512]{0,1:T(8,128)(2,1)S(1)} fusion(s32[]{:T(128)S(6)} %select_n.27, bf16[1024,512]{0,1:T(8,128)(2,1)} %all-gather.2.cloned.1.call-done, bf16[1024,512]{0,1:T(8,128)(2,1)S(1)} %collective-permute-done.3), kind=kLoop, calls=%fused_computation.3 | loop fusion | flops 2097152 | bytes 3145732 | tf_op jit(solution)/shard_map/concatenate | solution.py:32
  55.6 0.0 copy-done
  55.6 1.1 convolution_bitcast_fusion
  56.7 0.0 all-reduce.2.cloned.1.call-update
  56.7 0.0 reduce-scatter.2.cloned.1.call-start
  56.8 0.1 dynamic-slice_bitcast_fusion
  56.9 41.4 %all-reduce.2.cloned.1.call-done = f32[4,128,128]{1,2,0:T(8,128)} async-done(((f32[4,128,128]{1,2,0:T(8,128)}), f32[4,128,128]{1,2,0:T(8,128)}) %all-reduce.2.cloned.1.call-update) | async-done | bytes 262160 | tf_op jit(solution)/shard_map/psum | solution.py:39
  98.3 1.2 fusion.3
  99.6 0.2 copy.12
  99.8 0.1 broadcast_in_dim.11
  99.9 0.1 constant_dynamic-update-slice_fusion.8
  99.9 0.0 copy-start.1
  100.0 1.5 %collective-permute-start.5 = (f32[256,512]{1,0:T(8,128)S(1)}, f32[256,512]{1,0:T(8,128)S(1)}, u32[]{:S(2)}, u32[]{:S(2)}) collective-permute-start(f32[256,512]{1,0:T(8,128)S(1)} %slice.29), channel_id=1, source_target_pairs={{0,16},{1,17},{2,18},{3,19},{4,20},{5,21},{6,22},{7,23},{8,24},{9,... | collective-permute-start | bytes 1572872 | tf_op jit(solution)/shard_map/ppermute | solution.py:10
  101.5 0.6 compare_reduce_fusion
  102.1 0.0 collective-permute-done.4
  102.1 0.6 fusion.2
  102.7 0.0 copy-done.1
  102.7 0.4 fusion.4
  103.1 0.2 copy.15
  103.3 0.0 collective-permute-done.5
  103.3 1.6 %fusion.1 = f32[256,512]{1,0:T(8,128)} fusion(f32[256,512]{1,0:T(8,128)S(1)} %collective-permute-done.5, f32[256,512]{1,0:T(8,128)S(1)} %copy.15, f32[256,1024]{1,0:T(8,128)S(1)} %constant_dynamic-update-slice_fusion.8, pred[]{:T(512)} %compare_reduce_fusion), kind=kLoop, calls=%fused_computation.5 | loop fusion | flops 393216 | bytes 2097153 | tf_op jit(solution)/shard_map/add | solution.py:62
  104.9 0.0 reduce-scatter.2.cloned.1.call-update
  104.9 22.0 %reduce-scatter.2.cloned.1.call-done = f32[256,128]{1,0:T(8,128)} async-done(((f32[256,512]{1,0:T(8,128)}), f32[256,128]{1,0:T(8,128)}) %reduce-scatter.2.cloned.1.call-update) | async-done | bytes 131088 | tf_op jit(solution)/shard_map/reduce_scatter | solution.py:63
  (11 shorter events, 0.1 us)
Async XLA Ops:
  6.5 46.7 %copy-start.2 = (s32[128]{0:T(128)S(1)}, s32[128]{0:T(128)}, u32[]{:S(2)}) copy-start(s32[128]{0:T(128)} %param.7) | copy-start | bytes 1540
  6.5 34.5 %all-gather.2.cloned.1.call-start = ((), (), s32[]{:S(2)}) async-start(), calls=%async_computation.1 | async-start | bytes 1310720 | tf_op jit(solution)/shard_map/all_gather | solution.py:28
  8.4 90.0 %all-reduce.2.cloned.1.call-start = ((), (), s32[]{:S(2)}) async-start(), calls=%async_computation.2 | async-start | bytes 524288 | tf_op jit(solution)/shard_map/psum | solution.py:39
  8.4 34.0 %collective-permute-start = (s32[128]{0:T(128)}, s32[128]{0:T(128)S(1)}, u32[]{:S(2)}, u32[]{:S(2)}) collective-permute-start(s32[128]{0:T(128)} %param.7), channel_id=1, source_target_pairs={{0,4},{4,8},{8,12},{12,0},{1,5},{5,9},{9,13},{13,1},{2,6},{6,10},{... | collective-permute-start | bytes 1544 | tf_op jit(solution)/shard_map/ppermute | solution.py:23
  28.7 73.4 %collective-permute-start.4 = (bf16[256,512]{0,1:T(8,128)(2,1)S(1)}, bf16[256,512]{0,1:T(8,128)(2,1)S(1)}, u32[]{:S(2)}, u32[]{:S(2)}) collective-permute-start(bf16[256,512]{0,1:T(8,128)(2,1)S(1)} %all_gather.7), channel_id=1, source_target_pairs={{16,0},{17,1},{18,2},{19,3},{20,4},{21,5},{22,6},{23,7},{24,8},{25... | collective-permute-start | bytes 786440 | tf_op jit(solution)/shard_map/ppermute | solution.py:10
  41.0 12.3 %collective-permute-start.3 = (bf16[1024,512]{0,1:T(8,128)(2,1)}, bf16[1024,512]{0,1:T(8,128)(2,1)S(1)}, u32[]{:S(2)}, u32[]{:S(2)}) collective-permute-start(bf16[1024,512]{0,1:T(8,128)(2,1)} %all-gather.2.cloned.1.call-done), channel_id=1, source_target_pairs={{16,0},{17,1},{18,2},{19,3},{20,4},{21,5},{22,6},{23,7},{24,8},{25... | collective-permute-start | bytes 3145736 | tf_op jit(solution)/shard_map/ppermute | solution.py:10
  42.4 5.4 %collective-permute-start.1 = (s32[128]{0:T(128)S(1)}, s32[128]{0:T(128)S(1)}, u32[]{:S(2)}, u32[]{:S(2)}) collective-permute-start(s32[128]{0:T(128)S(1)} %collective-permute-done), channel_id=1, source_target_pairs={{0,4},{4,8},{8,12},{12,0},{1,5},{5,9},{9,13},{13,1},{2,6},{6,10},{... | collective-permute-start | bytes 1544 | tf_op jit(solution)/shard_map/ppermute | solution.py:23
  47.8 5.4 %collective-permute-start.2 = (s32[128]{0:T(128)S(1)}, s32[128]{0:T(128)S(1)}, u32[]{:S(2)}, u32[]{:S(2)}) collective-permute-start(s32[128]{0:T(128)S(1)} %collective-permute-done.1), channel_id=1, source_target_pairs={{0,4},{4,8},{8,12},{12,0},{1,5},{5,9},{9,13},{13,1},{2,6},{6,10},{... | collective-permute-start | bytes 1544 | tf_op jit(solution)/shard_map/ppermute | solution.py:23
  53.2 2.3 %copy-start = (bf16[1024,512]{0,1:T(8,128)(2,1)S(1)}, bf16[1024,512]{0,1:T(8,128)(2,1)}, u32[]{:S(2)}) copy-start(bf16[1024,512]{0,1:T(8,128)(2,1)} %all-gather.2.cloned.1.call-done) | copy-start | bytes 3145732
  56.7 70.2 %reduce-scatter.2.cloned.1.call-start = ((), (), s32[]{:S(2)}) async-start(), calls=%async_computation.3 | async-start | bytes 655360 | tf_op jit(solution)/shard_map/reduce_scatter | solution.py:63
  99.9 2.8 %copy-start.1 = (f32[4,128,128]{1,2,0:T(8,128)S(1)}, f32[4,128,128]{1,2,0:T(8,128)}, u32[]{:S(2)}) copy-start(f32[4,128,128]{1,2,0:T(8,128)} %all-reduce.2.cloned.1.call-done) | copy-start | bytes 786436
  100.0 3.3 %collective-permute-start.5 = (f32[256,512]{1,0:T(8,128)S(1)}, f32[256,512]{1,0:T(8,128)S(1)}, u32[]{:S(2)}, u32[]{:S(2)}) collective-permute-start(f32[256,512]{1,0:T(8,128)S(1)} %slice.29), channel_id=1, source_target_pairs={{0,16},{1,17},{2,18},{3,19},{4,20},{5,21},{6,22},{7,23},{8,24},{9,... | collective-permute-start | bytes 1572872 | tf_op jit(solution)/shard_map/ppermute | solution.py:10
Sparse Core Ops, SparseCore 0:
  8.9 32.0 all-gather.1
  56.9 41.4 all-reduce.1
  105.1 21.8 reduce-scatter.1
